TPU v7x, 256 devices: a whole 4x4x8 slice. The times are simulated.
256 devices in a mesh: exp: 32 (over y, z_hi, core), hid: 8 (over z_lo, x).
Axes of the slice: x: 4, y: 4, z: 8 (z_hi: 4, z_lo: 2; z = z_hi * 2 + z_lo), core: 2. Of those that a mesh axis runs over, the one named last changes fastest.
Arguments:
- tokens: bfloat16 [1024, 2048], P(('exp', 'hid')), may hold values from -6 to 6
- grad_out: bfloat16 [1024, 2048], P(('exp', 'hid')), may hold values from -3 to 3
- router_logits: float32 [1024, 128], P(('exp', 'hid')), may hold values from -12 to 330
- selected: int32 [1024, 8], P(('exp', 'hid')), may hold values from 0 to 127, as said below
- router_w: bfloat16 [2048, 128], replicated, may hold values from -0.59765625 to 0.59765625
- w_gate: bfloat16 [256, 2048, 384], P(('exp', 'hid')), may hold values from -0.125 to 0.125
- w_up: bfloat16 [256, 2048, 384], P(('exp', 'hid')), may hold values from -0.125 to 0.125
- w_down: bfloat16 [256, 384, 2048], P(('exp', 'hid')), may hold values from -0.21875 to 0.21875
Outputs:
- x_grad: bfloat16 [1024, 2048], P(('exp', 'hid'))
- router_grad: float32 [2048, 128], P(('exp', 'hid'))
Inputs may be any that keep to these rules, and one draw needn't show every extreme that they name: `selected`: each row names 8 different experts; within each aligned block of 32 rows (the tokens of one index of exp) no expert is named by more than 4 rows, and in every block some expert is named by exactly 4 rows.
All inputs are finite; a program needn't handle non-finite values.
Results may differ from a plain program's by a relative error of at most 0.0075.
Values may be sent and summed in bfloat16 or wider, within the bound.
A program may use at most 64 MiB of HBM per device.

v0:
```python
import jax
import jax.numpy as jnp
from jax import lax
from jax.sharding import PartitionSpec as P


def softmax_rows(values):
    top_val = jnp.max(values, axis=-1, keepdims=True)
    raised = jnp.exp(values - top_val)
    return raised / jnp.sum(raised, axis=-1, keepdims=True)


def combine_table(logits, chosen, expert_count):
    picked = jnp.take_along_axis(logits, chosen, axis=1)
    weights = softmax_rows(picked)
    expert_ids = jnp.arange(expert_count, dtype=jnp.int32)
    matched = (chosen[:, :, None] == expert_ids[None, None, :]).astype(jnp.float32)
    return jnp.sum(weights[:, :, None] * matched, axis=1).astype(jnp.bfloat16)


def unit_terms(x_rows, g_rows, c_rows, w_gate, w_up, w_down, unit_pick):
    gate_pre = jnp.einsum("td,udf->utf", x_rows, w_gate, preferred_element_type=jnp.float32)
    up_pre = jnp.einsum("td,udf->utf", x_rows, w_up, preferred_element_type=jnp.float32)
    back_grad = jnp.einsum("td,ufd->utf", g_rows, w_down, preferred_element_type=jnp.float32)
    sig_gate = jax.nn.sigmoid(gate_pre)
    act_gate = gate_pre * sig_gate
    score_part = jnp.sum(act_gate * up_pre * back_grad, axis=2).T
    column_rows = jnp.dot(c_rows, unit_pick, preferred_element_type=jnp.float32)
    weighted = column_rows.T[:, :, None] * back_grad
    grad_gate = (weighted * up_pre * sig_gate * (1.0 + gate_pre * (1.0 - sig_gate))).astype(
        jnp.bfloat16
    )
    grad_up = (weighted * act_gate).astype(jnp.bfloat16)
    input_part = jnp.einsum("utf,udf->td", grad_gate, w_gate, preferred_element_type=jnp.float32)
    input_part = input_part + jnp.einsum(
        "utf,udf->td", grad_up, w_up, preferred_element_type=jnp.float32
    )
    return (score_part, input_part, column_rows)


def on_device(tokens, grad_out, router_logits, selected, router_w, w_gate, w_up, w_down):
    tok_local, model_width = tokens.shape
    unit_count = w_gate.shape[0]
    expert_count = router_logits.shape[1]
    spread_exp = lax.axis_size("exp")
    spread_hid = lax.axis_size("hid")
    own_block = lax.axis_index(("exp", "hid"))
    unit_expert = (own_block * unit_count + jnp.arange(unit_count, dtype=jnp.int32)) // 2
    expert_ids = jnp.arange(expert_count, dtype=jnp.int32)
    unit_pick = (expert_ids[:, None] == unit_expert[None, :]).astype(jnp.bfloat16)
    combine = combine_table(router_logits, selected, expert_count)
    score_part, input_part, column_rows = unit_terms(
        lax.all_gather(tokens, ("exp", "hid"), axis=0, tiled=True),
        lax.all_gather(grad_out, ("exp", "hid"), axis=0, tiled=True),
        lax.all_gather(combine, ("exp", "hid"), axis=0, tiled=True),
        w_gate,
        w_up,
        w_down,
        unit_pick,
    )
    input_all = input_part
    used_all = column_rows
    scores, input_all, used_all = (score_part, input_all, used_all)
    input_sum = lax.psum_scatter(input_all, ("exp", "hid"), scatter_dimension=0, tiled=True)
    shaped = scores.reshape(spread_exp, spread_hid, tok_local, 1, unit_count)
    arrived = lax.all_to_all(
        lax.all_to_all(shaped, "exp", split_axis=0, concat_axis=3, tiled=True),
        "hid",
        split_axis=1,
        concat_axis=4,
        tiled=True,
    )
    expert_scores = jnp.sum(arrived.reshape(tok_local, expert_count, 2), axis=2)
    probs_all = softmax_rows(router_logits)
    mean_score = jnp.sum(probs_all * expert_scores, axis=1, keepdims=True)
    logit_grad = (probs_all * (expert_scores - mean_score)).astype(jnp.bfloat16)
    router_grad = lax.psum_scatter(
        jnp.einsum("tc,te->ce", tokens, logit_grad, preferred_element_type=jnp.float32),
        ("exp", "hid"),
        scatter_dimension=0,
        tiled=True,
    )
    router_part = jnp.einsum("te,de->td", logit_grad, router_w, preferred_element_type=jnp.float32)
    x_grad = (input_sum + router_part).astype(jnp.bfloat16)
    return (x_grad, router_grad)


def solution(mesh):
    placed = (
        P(("exp", "hid"), None),
        P(("exp", "hid"), None),
        P(("exp", "hid"), None),
        P(("exp", "hid"), None),
        P(),
        P(("exp", "hid"), None, None),
        P(("exp", "hid"), None, None),
        P(("exp", "hid"), None, None),
    )
    return jax.shard_map(
        on_device,
        mesh=mesh,
        in_specs=placed,
        out_specs=(P(("exp", "hid"), None), P(("exp", "hid"), None)),
        check_vma=False,
    )
```

profile of v0, /device:TPU:97, one launch (start us, length us, event | category | flops | bytes accessed | tf_op | source)
XLA Modules:
  0.0 1772.1 jit_solution(1746545466882803414)
XLA Ops:
  7.2 0.0 copy-start
  7.2 0.0 all-gather.8.cloned.1.call-start
  7.2 0.7 all-gather.8.cloned.1.call-update
  7.9 0.0 all-gather.6.cloned.1.call-start
  8.0 0.7 all-gather.6.cloned.1.call-update
  8.7 0.7 bitcast_or_fusion
  9.4 0.1 reshape.86
  9.5 1.4 gather_fusion
  10.9 0.1 reshape.89
  11.0 0.1 reduce_max.19
  11.1 0.2 fusion.30
  11.3 0.1 fusion.35
  11.4 0.2 fusion.28
  11.6 0.1 fusion.27
  11.7 0.1 select_reduce_fusion
  11.8 561.5 %all-gather = bf16[256,4,128]{2,1,0:T(4,128)(2,1)S(1)} all-gather(bf16[1,4,128]{2,1,0:T(4,128)(2,1)S(1)} %bitcast.132), channel_id=1, replica_groups=mesh['exp'=32,'hid'=8] {'exp','hid'}, dimensions={0}, use_global_device_ids=true | all-gather | bytes 263168 | tf_op jit(solution)/shard_map/all_gather | solution.py:55
  573.3 0.2 fusion.24
  573.5 150.6 %all-gather.8.cloned.1.call-done = bf16[256,4,2048]{2,1,0:T(4,128)(2,1)} async-done(((bf16[1,4,2048]{2,1,0:T(4,128)(2,1)}), bf16[256,4,2048]{2,1,0:T(4,128)(2,1)}) %all-gather.8.cloned.1.call-update) | async-done | bytes 4194320 | tf_op jit(solution)/shard_map/all_gather | solution.py:53
  724.0 6.9 reshape.102
  731.0 4.2 fusion.11
  735.1 3.0 fusion.14
  738.1 693.5 %all-gather.6.cloned.1.call-done = bf16[256,4,2048]{2,1,0:T(4,128)(2,1)} async-done(((bf16[1,4,2048]{2,1,0:T(4,128)(2,1)}), bf16[256,4,2048]{2,1,0:T(4,128)(2,1)}) %all-gather.6.cloned.1.call-update) | async-done | bytes 4194320 | tf_op jit(solution)/shard_map/all_gather | solution.py:54
  1431.6 6.9 reshape.100
  1438.5 6.2 fusion.1
  1444.8 0.1 reshape_transpose.3
  1444.9 0.9 copy.38
  1445.8 7.2 all-to-all-start
  1453.0 7.9 fusion.9
  1460.8 0.2 all-to-all-done
  1461.0 0.1 copy.39
  1461.1 0.5 broadcast.72
  1461.6 0.7 reduce.1
  1462.3 0.7 reshape.107
  1463.0 4.0 all-to-all-start.1
  1467.0 10.0 convolution_add_fusion
  1477.0 0.7 reduce.2
  1477.7 0.1 reshape.108
  1477.8 0.1 copy.41
  1477.9 0.2 reduce_sum.58
  1478.1 0.1 copy.43
  1478.2 0.2 multiply_reduce_fusion
  1478.4 0.1 multiply_convert_fusion.1
  1478.5 1.4 convolution_bitcast_fusion
  1479.9 0.0 all-reduce.5.cloned.1.call-update
  1479.9 282.4 %all-reduce.5.cloned.1.call-done = (f32[1024,2048]{1,0:T(8,128)}, f32[2048,128]{0,1:T(8,128)}) async-done(((f32[1024,2048]{1,0:T(8,128)}, f32[2048,128]{0,1:T(8,128)}), (f32[1024,2048]{1,0:T(8,128)}, f32[2048,128]{0,1:T(8,128)})) %all-reduce.5.cloned.1.call-update) | async-done | bytes 9437200
  1762.3 0.9 constant_dynamic-slice_fusion
  1763.2 0.7 copy.44
  1763.9 1.7 fusion
  (16 shorter events, 0.1 us)
Async XLA Ops:
  7.2 723.8 %copy-start = (bf16[1,2048,384]{2,1,0:T(8,128)(2,1)S(1)}, bf16[1,2048,384]{2,1,0:T(8,128)(2,1)}, u32[]{:S(2)}) copy-start(bf16[1,2048,384]{2,1,0:T(8,128)(2,1)} %param.13) | copy-start | bytes 4718596
  7.2 4.1 copy-start.6
  7.2 3.8 copy-start.1
  7.2 716.8 %all-gather.8.cloned.1.call-start = ((), (), s32[]{:S(2)}) async-start(), calls=%async_computation.3 | async-start | bytes 4210688 | tf_op jit(solution)/shard_map/all_gather | solution.py:53
  7.9 1423.7 %all-gather.6.cloned.1.call-start = ((), (), s32[]{:S(2)}) async-start(), calls=%async_computation.2 | async-start | bytes 4210688 | tf_op jit(solution)/shard_map/all_gather | solution.py:54
  730.9 4.2 copy-start.2
  730.9 4.2 copy-start.3
  1445.8 15.2 all-to-all-start
  1463.0 14.0 all-to-all-start.1
  1467.0 11.5 copy-start.5
  1467.0 295.3 %all-reduce.5.cloned.1.call-start = ((), (), s32[]{:S(2)}) async-start(), calls=%async_computation.4 | async-start | bytes 18874368
  1479.9 284.1 %copy-start.4 = (bf16[2048,128]{1,0:T(8,128)(2,1)S(1)}, bf16[2048,128]{1,0:T(8,128)(2,1)}, u32[]{:S(2)}) copy-start(bf16[2048,128]{1,0:T(8,128)(2,1)} %param.12) | copy-start | bytes 1572868
Sparse Core Ops, SparseCore 0:
  9.9 714.0 all-gather.7
  725.9 705.6 all-gather.5
  1480.0 282.2 all-reduce.4
where the time goes:
time: 1770 us
  waiting for transfers between devices  1130 us (64%)
  blocking collectives  562 us (32%)
  matrix products  34.6 us (2%)
  local copies, waits for them, and re-layouts  19.6 us (1%)
    all_gather x1, waiting for transfers between devices, on_device(): lax.all_gather(grad_out, ('exp', 'hid'), axis=0, tiled=True)  693 us
    all_gather x1, blocking collectives, on_device(): lax.all_gather(combine, ('exp', 'hid'), axis=0, tiled=True)  562 us
    unnamed x4, waiting for transfers between devices  284 us
    all_gather x1, waiting for transfers between devices, on_device(): lax.all_gather(tokens, ('exp', 'hid'), axis=0, tiled=True)  151 us
  transfers between devices with their start and end apart: 5, of which 4 were waited for; matrix products, arithmetic and copies ran while one was open for 2% of the time, Pallas kernels for 0%

commit v1 on v0

--- a/solution.py
+++ b/solution.py
@@ -50,7 +50,12 @@
     unit_pick = (expert_ids[:, None] == unit_expert[None, :]).astype(jnp.bfloat16)
     combine = combine_table(router_logits, selected, expert_count)
     score_part, input_part, column_rows = unit_terms(
-        lax.all_gather(tokens, ("exp", "hid"), axis=0, tiled=True),
+        jnp.concatenate(
+            lax.all_to_all(
+                jnp.stack([tokens] * lax.axis_size(("exp", "hid"))), ("exp", "hid"), 0, 0
+            ),
+            axis=0,
+        ),
         lax.all_gather(grad_out, ("exp", "hid"), axis=0, tiled=True),
         lax.all_gather(combine, ("exp", "hid"), axis=0, tiled=True),
         w_gate,

time: 1770 us -> 1100 us (0.62)
  waiting for transfers between devices: 1130 us -> 365 us
  blocking collectives: 562 us -> 633 us
    all_gather x1, waiting for transfers between devices: 693 us -> 82.3 us  [on_device(): lax.all_gather(grad_out, ('exp', 'hid'), axis=0, tiled=True)]
    all_gather x1 -> x0, waiting for transfers between devices: 151 us -> none  [on_device(): lax.all_gather(tokens, ('exp', 'hid'), axis=0, tiled=True)]
    all_gather x1, blocking collectives: 562 us -> 633 us  [on_device(): lax.all_gather(combine, ('exp', 'hid'), axis=0, tiled=True)]
    unnamed x4 -> x3, waiting for transfers between devices: 284 us -> 283 us
  transfers between devices with their start and end apart: 5 -> 5, of which waited for: 4 -> 2; matrix products, arithmetic and copies ran while one was open for 2% -> 3% of each run, Pallas kernels for 0% -> 0%
where the time goes in v1:
time: 1100 us
  blocking collectives  633 us (58%)
  waiting for transfers between devices  365 us (33%)
  matrix products  34.6 us (3%)
  starting transfers between devices  26.7 us (2%)
  local copies, waits for them, and re-layouts  23.9 us (2%)
  between operations  14.2 us (1%)
    all_gather x1, blocking collectives, on_device(): lax.all_gather(combine, ('exp', 'hid'), axis=0, tiled=True)  633 us
    unnamed x3, waiting for transfers between devices  283 us
    all_gather x1, waiting for transfers between devices, on_device(): lax.all_gather(grad_out, ('exp', 'hid'), axis=0, tiled=True)  82.3 us
  transfers between devices with their start and end apart: 5, of which 2 were waited for; matrix products, arithmetic and copies ran while one was open for 3% of the time, Pallas kernels for 0%

profile of v1, /device:TPU:97, one launch (start us, length us, event | category | flops | bytes accessed | tf_op | source)
XLA Modules:
  0.0 1100.2 jit_solution(15828011046348913139)
XLA Ops:
  7.2 0.0 copy-start
  7.2 4.9 stack.2
  12.1 15.3 %all-to-all-start = ((bf16[256,4,2048]{2,1,0:T(4,128)(2,1)}), bf16[256,4,2048]{2,1,0:T(4,128)(2,1)}, u32[]{:S(2)}, u32[]{:S(2)}) async-start(bf16[256,4,2048]{2,1,0:T(4,128)(2,1)} %stack.2), calls=%async_computation | async-start | bytes 8388608 | tf_op jit(solution)/shard_map/all_to_all | solution.py:54
  27.5 0.0 all-gather.4.cloned.1.call-start
  27.5 0.7 all-gather.4.cloned.1.call-update
  28.2 0.1 reshape.92
  28.3 0.8 gather_fusion
  29.1 0.1 reshape.95
  29.2 0.1 reduce_max.19
  29.3 0.2 fusion.30
  29.5 0.1 fusion.35
  29.6 0.2 fusion.28
  29.8 0.1 fusion.27
  29.8 0.1 select_reduce_fusion
  29.9 632.8 %all-gather = bf16[256,4,128]{2,1,0:T(4,128)(2,1)S(1)} all-gather(bf16[1,4,128]{2,1,0:T(4,128)(2,1)S(1)} %bitcast.130), channel_id=1, replica_groups=mesh['exp'=32,'hid'=8] {'exp','hid'}, dimensions={0}, use_global_device_ids=true | all-gather | bytes 263168 | tf_op jit(solution)/shard_map/all_gather | solution.py:60
  662.8 0.2 fusion.24
  662.9 0.0 all-to-all-done
  662.9 7.0 reshape.87
  669.9 4.2 fusion.11
  674.1 3.0 fusion.14
  677.1 82.3 %all-gather.4.cloned.1.call-done = bf16[256,4,2048]{2,1,0:T(4,128)(2,1)} async-done(((bf16[1,4,2048]{2,1,0:T(4,128)(2,1)}), bf16[256,4,2048]{2,1,0:T(4,128)(2,1)}) %all-gather.4.cloned.1.call-update) | async-done | bytes 4194320 | tf_op jit(solution)/shard_map/all_gather | solution.py:59
  759.4 6.9 reshape.106
  766.3 6.2 fusion.1
  772.6 0.1 reshape_transpose.3
  772.7 0.9 copy.38
  773.6 5.2 all-to-all-start.1
  778.8 7.9 fusion.9
  786.6 0.0 all-to-all-done.1
  786.7 0.1 copy.39
  786.8 0.5 broadcast.74
  787.3 0.7 reduce.1
  788.0 0.7 reshape.111
  788.7 6.1 all-to-all-start.2
  794.8 10.0 convolution_add_fusion
  804.9 0.0 all-to-all-done.2
  804.9 0.7 reduce.2
  805.5 0.1 reshape.112
  805.6 0.1 copy.41
  805.8 0.2 reduce_sum.58
  805.9 0.1 copy.43
  806.0 0.2 multiply_reduce_fusion
  806.2 0.1 multiply_convert_fusion.1
  806.3 1.4 convolution_bitcast_fusion
  807.7 0.0 all-reduce.5.cloned.1.call-update
  807.7 282.3 %all-reduce.5.cloned.1.call-done = (f32[1024,2048]{1,0:T(8,128)}, f32[2048,128]{0,1:T(8,128)}) async-done(((f32[1024,2048]{1,0:T(8,128)}, f32[2048,128]{0,1:T(8,128)}), (f32[1024,2048]{1,0:T(8,128)}, f32[2048,128]{0,1:T(8,128)})) %all-reduce.5.cloned.1.call-update) | async-done | bytes 9437200
  1090.0 0.9 constant_dynamic-slice_fusion
  1091.0 0.7 copy.44
  1091.6 1.7 fusion
  (16 shorter events, 0.1 us)
Async XLA Ops:
  7.2 662.7 %copy-start = (bf16[1,2048,384]{2,1,0:T(8,128)(2,1)S(1)}, bf16[1,2048,384]{2,1,0:T(8,128)(2,1)}, u32[]{:S(2)}) copy-start(bf16[1,2048,384]{2,1,0:T(8,128)(2,1)} %param.13) | copy-start | bytes 4718596
  12.1 16.1 %copy-start.6 = (s32[4,8]{1,0:T(4,128)S(1)}, s32[4,8]{1,0:T(4,128)}, u32[]{:S(2)}) copy-start(s32[4,8]{1,0:T(4,128)} %param.11) | copy-start | bytes 388
  12.1 16.2 %copy-start.1 = (f32[4,128]{1,0:T(4,128)S(1)}, f32[4,128]{1,0:T(4,128)}, u32[]{:S(2)}) copy-start(f32[4,128]{1,0:T(4,128)} %param.10) | copy-start | bytes 6148
  12.1 650.8 %all-to-all-start = ((bf16[256,4,2048]{2,1,0:T(4,128)(2,1)}), bf16[256,4,2048]{2,1,0:T(4,128)(2,1)}, u32[]{:S(2)}, u32[]{:S(2)}) async-start(bf16[256,4,2048]{2,1,0:T(4,128)(2,1)} %stack.2), calls=%async_computation | async-start | bytes 8388608 | tf_op jit(solution)/shard_map/all_to_all | solution.py:54
  27.5 732.0 %all-gather.4.cloned.1.call-start = ((), (), s32[]{:S(2)}) async-start(), calls=%async_computation.3 | async-start | bytes 4210688 | tf_op jit(solution)/shard_map/all_gather | solution.py:59
  669.9 4.2 copy-start.2
  669.9 4.2 copy-start.3
  773.6 13.1 %all-to-all-start.1 = ((f32[32,8,4,1,1]{1,2,4,3,0:T(4,128)}), f32[32,8,4,1,1]{1,2,4,3,0:T(4,128)S(1)}, u32[]{:S(2)}, u32[]{:S(2)}) async-start(f32[32,8,4,1,1]{1,2,4,3,0:T(4,128)} %copy.38), calls=%async_computation.1 | async-start | bytes 131072 | tf_op jit(solution)/shard_map/all_to_all | solution.py:72
  788.7 16.2 %all-to-all-start.2 = ((f32[8,1,128]{2,1,0:T(1,128)}), f32[8,1,128]{2,1,0:T(1,128)S(1)}, u32[]{:S(2)}, u32[]{:S(2)}) async-start(f32[8,1,128]{2,1,0:T(1,128)} %reshape.111), calls=%async_computation.2 | async-start | bytes 8192 | tf_op jit(solution)/shard_map/all_to_all | solution.py:71
  794.8 11.5 %copy-start.5 = (bf16[4,2048]{1,0:T(4,128)(2,1)S(1)}, bf16[4,2048]{1,0:T(4,128)(2,1)}, u32[]{:S(2)}) copy-start(bf16[4,2048]{1,0:T(4,128)(2,1)} %param.8) | copy-start | bytes 49156
  794.8 295.2 %all-reduce.5.cloned.1.call-start = ((), (), s32[]{:S(2)}) async-start(), calls=%async_computation.4 | async-start | bytes 18874368
  807.7 284.0 %copy-start.4 = (bf16[2048,128]{1,0:T(8,128)(2,1)S(1)}, bf16[2048,128]{1,0:T(8,128)(2,1)}, u32[]{:S(2)}) copy-start(bf16[2048,128]{1,0:T(8,128)(2,1)} %param.12) | copy-start | bytes 1572868
Sparse Core Ops, SparseCore 0:
  30.2 729.2 all-gather.3
  807.8 282.1 all-reduce.4
